TPU v7x, 256 devices: a whole 4x4x8 slice. The times are simulated.
256 devices in a mesh: filt: 2 (over core), row: 4 (over x), col: 32 (over z, y).
Axes of the slice: x: 4, y: 4, z: 8, core: 2. Of those that a mesh axis runs over, the one named last changes fastest.
Arguments:
- particles: bfloat16 [24576, 256], P(('filt', 'row', 'col')), parts along dimension 0, may hold values from -6 to 6
- cotangent: bfloat16 [24576, 256], P(('filt', 'row', 'col')), parts along dimension 0, may hold values from -3 to 3
- row_potential: bfloat16 [24576], P(('filt', 'row', 'col')), parts along dimension 0, may hold values from -0.099609375 to 0.099609375
- col_potential: bfloat16 [24576], P(('filt', 'row', 'col')), parts along dimension 0, may hold values from -0.099609375 to 0.099609375
- weights: bfloat16 [24576], P(('filt', 'row', 'col')), parts along dimension 0, may hold values from 0.5 to 18
Outputs:
- grad_particles: bfloat16 [24576, 256], P(('filt', 'row', 'col')), parts along dimension 0
- grad_weights: float32 [24576], P(('filt', 'row', 'col')), parts along dimension 0
There are 2 independent parts, one for each index of `filt`. A program takes and returns all parts, laid end to end along the dimension named above; each array names one. Nothing has to cross between parts.
All inputs are finite; a program needn't handle non-finite values.
Results may differ from a plain program's by a relative error of at most 0.02.
Values may be sent and summed in bfloat16 or wider, within the bound.
No kernel may reach another device: no remote copies, remote signals or barrier semaphores. Data moves between devices by JAX's collectives and lax.ppermute only.
A program may use at most 64 MiB of HBM per device.

v0:
```python
import jax
import jax.numpy as jnp
from jax import lax
from jax.sharding import PartitionSpec as P

ITERS = 4
EPS = 0.09


def local(particles, cotangent, row_potential, col_potential, weights):
    row_parts, row_fpot, row_wts = (
        lax.all_gather(particles, "col", axis=0, tiled=True),
        lax.all_gather(row_potential, "col", axis=0, tiled=True),
        lax.all_gather(weights, "col", axis=0, tiled=True),
    )
    col_parts, col_grads, col_gpot = (
        lax.all_gather(particles, "row", axis=0, tiled=True),
        lax.all_gather(cotangent, "row", axis=0, tiled=True),
        lax.all_gather(col_potential, "row", axis=0, tiled=True),
    )
    own = particles.shape[0]
    width = particles.shape[1]
    rows = row_parts.shape[0]
    cols = col_parts.shape[0]
    blk = 512
    count = rows // blk
    row_float = row_parts.astype(jnp.float32)
    row_sq = jnp.sum(row_float * row_float, axis=1)
    col_float = col_parts.astype(jnp.float32)
    col_sq = jnp.sum(col_float * col_float, axis=1)
    fpot = row_fpot.astype(jnp.float32)
    gpot = col_gpot.astype(jnp.float32)
    stacked = jnp.concatenate([col_parts, col_grads], axis=0)
    items = (
        row_parts.reshape(count, blk, width),
        fpot.reshape(count, blk),
        row_sq.reshape(count, blk),
    )

    def plan_from(cross, pot_blk, sq_blk):
        cost = (sq_blk[:, None] + col_sq[None, :] - 2.0 * cross) / (2.0 * width)
        return jnp.exp((pot_blk[:, None] + gpot[None, :] - cost) / EPS)

    def plan_only(part_blk, pot_blk, sq_blk):
        cross = jnp.einsum("rd,cd->rc", part_blk, col_parts, preferred_element_type=jnp.float32)
        return plan_from(cross, pot_blk, sq_blk)

    def first(carry, item):
        part_blk, pot_blk, sq_blk = item
        both = jnp.einsum("rd,cd->rc", part_blk, stacked, preferred_element_type=jnp.float32)
        plan = plan_from(both[:, :cols], pot_blk, sq_blk)
        weighted = plan * both[:, cols:]
        return (
            (carry[0] + jnp.sum(plan, axis=0), carry[1] + jnp.sum(weighted, axis=0)),
            (jnp.sum(plan, axis=1), jnp.sum(weighted, axis=1)),
        )

    zeros_c = jnp.zeros((cols,), jnp.float32)
    (colmass_part, colph_part), (rowmass_part, rowph_part) = lax.scan(
        first, (zeros_c, zeros_c), items
    )
    rowmass, rowph = lax.psum((rowmass_part.reshape(rows), rowph_part.reshape(rows)), "col")
    colmass, colph = lax.psum((colmass_part, colph_part), "row")
    psi = zeros_c
    phi = jnp.zeros((rows,), jnp.float32)
    for step in range(ITERS):

        def apply_rows(carry, item):
            plan = plan_only(item[0], item[1], item[2])
            return (carry, jnp.dot(plan, psi, precision=lax.Precision.HIGHEST))

        unused, row_apply = lax.scan(apply_rows, jnp.zeros((), jnp.float32), items)
        row_total = lax.psum(row_apply.reshape(rows), "col")
        phi = -(rowph + row_total) / rowmass

        def apply_cols(acc, item):
            plan = plan_only(item[0], item[1], item[2])
            return (acc + jnp.dot(item[3], plan, precision=lax.Precision.HIGHEST), None)

        col_apply, unused_out = lax.scan(apply_cols, zeros_c, items + (phi.reshape(count, blk),))
        col_total = lax.psum(col_apply, "row")
        psi = -(colph + col_total) / colmass

    def last(acc, item):
        part_blk, pot_blk, sq_blk, phi_blk = item
        both = jnp.einsum("rd,cd->rc", part_blk, stacked, preferred_element_type=jnp.float32)
        plan = plan_from(both[:, :cols], pot_blk, sq_blk)
        mixed = plan * (both[:, cols:] + phi_blk[:, None] + psi[None, :])
        qrow = jnp.sum(mixed, axis=1)
        plan_bf = plan.astype(jnp.bfloat16)
        mixed_bf = mixed.astype(jnp.bfloat16)
        rowterm = jnp.dot(plan_bf, col_grads, preferred_element_type=jnp.float32)
        rowterm = rowterm + (
            jnp.dot(mixed_bf, col_parts, preferred_element_type=jnp.float32)
            - qrow[:, None] * part_blk.astype(jnp.float32)
        ) / (width * EPS)
        return (
            acc + jnp.einsum("rc,rd->cd", mixed_bf, part_blk, preferred_element_type=jnp.float32),
            rowterm,
        )

    col_acc, row_terms = lax.scan(
        last, jnp.zeros((cols, width), jnp.float32), items + (phi.reshape(count, blk),)
    )
    row_terms = row_terms.reshape(rows, width)
    start = lax.axis_index("col") * own
    summed = lax.psum(row_terms.astype(jnp.bfloat16), "col").astype(jnp.float32)
    row_own = lax.dynamic_slice_in_dim(summed, start, own, 0)
    col_own = lax.psum_scatter(
        col_acc.astype(jnp.bfloat16), "row", scatter_dimension=0, tiled=True
    ).astype(jnp.float32)
    grad_particles = (row_own + col_own / (width * EPS)).astype(jnp.bfloat16)
    phi_own = lax.dynamic_slice_in_dim(phi, start, own, 0)
    own_wts = weights.astype(jnp.float32)
    total, wphi = lax.psum((jnp.sum(own_wts), jnp.sum(own_wts * phi_own)), ("row", "col"))
    count_all = rows * lax.axis_size("row")
    grad_weights = -(count_all / total) * (phi_own - wphi / total)
    return (grad_particles, grad_weights)


def solution(mesh):
    return jax.shard_map(
        local,
        mesh=mesh,
        in_specs=(
            P(("filt", "row", "col"), None),
            P(("filt", "row", "col"), None),
            P(("filt", "row", "col")),
            P(("filt", "row", "col")),
            P(("filt", "row", "col")),
        ),
        out_specs=(P(("filt", "row", "col"), None), P(("filt", "row", "col"))),
        check_vma=False,
    )
```

profile of v0, /device:TPU:8, one launch (start us, length us, event | category | flops | bytes accessed | tf_op | source)
XLA Modules:
  0.0 1151.9 jit_solution(2241112115767740689)
XLA Ops:
  7.2 0.7 all-gather.2.cloned.1.call-update
  8.0 1.3 dynamic-slice
  9.9 0.9 dynamic-update-slice
  10.7 75.0 %all-reduce = bf16[3072]{0:T(1024)(128)(2,1)S(1)} all-reduce(bf16[3072]{0:T(1024)(128)(2,1)S(1)} %dynamic-update-slice), channel_id=1, replica_groups=mesh['filt'=2,'row'=4,'col'=32] {'col'}, use_global_device_ids=true, to_apply=%add | all-reduce | flops 3072 | bytes 12288
  85.8 1.3 dynamic-slice.1
  87.6 0.9 dynamic-update-slice.1
  88.5 10.5 all-reduce.1
  99.0 12.3 %all_gather.18 = bf16[384,256]{1,0:T(8,128)(2,1)S(1)} all-gather(bf16[96,256]{1,0:T(8,128)(2,1)} %param.25), channel_id=1, replica_groups=mesh['filt'=2,'row'=4,'col'=32] {'row'}, dimensions={0}, use_global_device_ids=true | all-gather | bytes 245760 | tf_op jit(solution)/shard_map/all_gather | solution.py:17
  111.3 12.3 %all_gather.19 = bf16[384,256]{1,0:T(8,128)(2,1)S(1)} all-gather(bf16[96,256]{1,0:T(8,128)(2,1)} %param.26), channel_id=1, replica_groups=mesh['filt'=2,'row'=4,'col'=32] {'row'}, dimensions={0}, use_global_device_ids=true | all-gather | bytes 245760 | tf_op jit(solution)/shard_map/all_gather | solution.py:18
  123.9 2.0 multiply_reduce_fusion
  125.9 7.0 while.118
  132.9 7.5 while.117
  133.4 0.8 fusion.226
  134.6 0.8 fusion.226
  135.9 0.8 fusion.226
  137.1 0.8 fusion.226
  138.4 0.8 fusion.226
  139.6 0.8 fusion.226
  140.5 139.2 %all-reduce.3 = (f32[3072]{0:T(1024)S(1)}, f32[3072]{0:T(1024)S(1)}, f32[3072]{0:T(1024)S(1)}) all-reduce(f32[3072]{0:T(1024)S(1)} %reshape.119, f32[3072]{0:T(1024)S(1)} %reshape.117, f32[3072]{0:T(1024)S(1)} %reshape.118), channel_id=1, replica_groups=mesh['filt'=2,'row'=4,'col'=32] {'col'}, use_global_device_ids=true, to_apply=%region_13.14 | all-reduce | flops 9216 | bytes 73728 | tf_op jit(solution)/shard_map/psum | solution.py:62
  279.7 5.8 while.119
  285.5 7.9 all-reduce.4
  294.0 7.5 while.124
  294.4 0.8 fusion.268
  295.6 0.8 fusion.268
  296.9 0.8 fusion.268
  298.1 0.8 fusion.268
  299.4 0.8 fusion.268
  300.6 0.8 fusion.268
  301.5 137.7 %psum.111 = f32[3072]{0:T(1024)S(1)} all-reduce(f32[3072]{0:T(1024)S(1)} %reshape.121), channel_id=1, replica_groups=mesh['filt'=2,'row'=4,'col'=32] {'col'}, use_global_device_ids=true, to_apply=%region_20.21 | all-reduce | flops 3072 | bytes 24576 | tf_op jit(solution)/shard_map/psum | solution.py:73
  439.2 5.8 while.120
  445.0 9.7 psum.112
  455.3 7.5 while.125
  455.7 0.8 fusion.274
  456.9 0.8 fusion.274
  458.2 0.8 fusion.274
  459.5 0.8 fusion.274
  460.7 0.8 fusion.274
  462.0 0.8 fusion.274
  462.8 137.7 %psum.113 = f32[3072]{0:T(1024)S(1)} all-reduce(f32[3072]{0:T(1024)S(1)} %reshape.123), channel_id=1, replica_groups=mesh['filt'=2,'row'=4,'col'=32] {'col'}, use_global_device_ids=true, to_apply=%region_26.27 | all-reduce | flops 3072 | bytes 24576 | tf_op jit(solution)/shard_map/psum | solution.py:73
  600.5 5.8 while.121
  606.3 7.7 psum.114
  614.7 7.5 while.126
  615.1 0.8 fusion.280
  616.3 0.8 fusion.280
  617.6 0.8 fusion.280
  618.8 0.8 fusion.280
  620.1 0.8 fusion.280
  621.3 0.8 fusion.280
  622.2 138.0 %psum.115 = f32[3072]{0:T(1024)S(1)} all-reduce(f32[3072]{0:T(1024)S(1)} %reshape.125), channel_id=1, replica_groups=mesh['filt'=2,'row'=4,'col'=32] {'col'}, use_global_device_ids=true, to_apply=%region_32.33 | all-reduce | flops 3072 | bytes 24576 | tf_op jit(solution)/shard_map/psum | solution.py:73
  760.2 5.8 while.122
  765.9 9.7 psum.116
  775.7 16.9 %while.123 = (s32[]{:T(128)}, f32[384,256]{1,0:T(8,128)S(1)}, bf16[6,512,256]{2,1,0:T(8,128)(2,1)}, f32[6,512]{1,0:T(8,128)S(1)}, f32[384]{0:T(512)S(1)}, /*inde...) while((s32[]{:T(128)}, f32[384,256]{1,0:T(8,128)S(1)}, ...), condition=%wide.region_38.39_spmd.clone, body=%wide.region_36.38_spmd.clone.sunk | while | flops 508100096 | bytes 9079975 | solution.py:102
  777.1 1.0 fusion.262
  779.9 1.0 fusion.262
  782.7 1.0 fusion.262
  785.5 1.0 fusion.262
  788.4 1.0 fusion.262
  791.2 1.0 fusion.262
  792.6 0.7 convert_element_type.46
  793.4 0.7 all-reduce.7.cloned.1.call-update
  794.1 0.7 convert_reduce_fusion
  794.8 346.5 %all-reduce.2 = (f32[]{:T(128)}, f32[]{:T(128)}) all-reduce(f32[]{:T(128)} %get-tuple-element.718, f32[]{:T(128)} %get-tuple-element.717), channel_id=1, replica_groups=mesh['filt'=2,'row'=4,'col'=32] {'row','col'}, use_global_device_ids=true, to_apply=%region_44.45 | all-reduce | flops 2 | bytes 16 | tf_op jit(solution)/shard_map/psum | solution.py:115
  1143.3 0.6 subtract_multiply_fusion
  1143.9 1.5 add_convert_fusion
  (306 shorter events, 52.6 us)
Async XLA Ops:
  7.2 116.7 %all-gather.2.cloned.1.call-start = ((), (), s32[]{:S(2)}) async-start(), calls=%async_computation.1 | async-start | bytes 1622016 | tf_op jit(solution)/shard_map/all_gather | solution.py:12
  7.9 1136.0 %reduce-scatter.2.cloned.1.call-start = ((), (), s32[]{:S(2)}) async-start(), calls=%async_computation.3 | async-start | bytes 245760 | tf_op jit(solution)/shard_map/reduce_scatter | solution.py:109
  123.8 2.1 copy-start
  293.4 0.6 copy-start.2
  454.7 0.6 copy-start.3
  614.1 0.6 copy-start.1
  792.6 1.5 copy-start.4
  793.4 350.6 %all-reduce.7.cloned.1.call-start = ((), (), s32[]{:S(2)}) async-start(), calls=%async_computation.2 | async-start | bytes 3145728 | tf_op jit(solution)/shard_map/psum | solution.py:107
Sparse Core Ops, SparseCore 0:
  10.6 78.8 all-gather.1
  793.5 18.2 reduce-scatter.1
  815.6 149.9 all-reduce.6
where the time goes:
time: 1150 us
  blocking collectives  1040 us (90%)
  matrix products  65.2 us (6%)
  between operations  17.3 us (2%)
  other arithmetic  12.4 us (1%)
    psum x3, blocking collectives, local(): row_total = lax.psum(row_apply.reshape(rows), 'col')  413 us
    psum x1, blocking collectives, local(): lax.psum((jnp.sum(own_wts), jnp.sum(own_wts * phi_own)), ('row', 'col'))  347 us
    psum x1, blocking collectives, local(): lax.psum((rowmass_part.reshape(rows), rowph_part.reshape(rows)), 'col')  139 us
    unnamed x2, blocking collectives  85.5 us
    psum x3, blocking collectives, local(): col_total = lax.psum(col_apply, 'row')  27.2 us
  transfers between devices with their start and end apart: 3, of which 0 were waited for; matrix products, arithmetic and copies ran while one was open for 0% of the time, Pallas kernels for 0%

commit v1 on v0

--- a/solution.py
+++ b/solution.py
@@ -70,7 +70,7 @@
             return (carry, jnp.dot(plan, psi, precision=lax.Precision.HIGHEST))
 
         unused, row_apply = lax.scan(apply_rows, jnp.zeros((), jnp.float32), items)
-        row_total = lax.psum(row_apply.reshape(rows), "col")
+        row_total = jnp.sum(lax.all_gather(row_apply.reshape(rows), "col"), axis=0)
         phi = -(rowph + row_total) / rowmass
 
         def apply_cols(acc, item):

time: 1150 us -> 931 us (0.81)
  blocking collectives: 1040 us -> 822 us
    psum x3 -> x0, blocking collectives: 413 us -> none  [local(): row_total = lax.psum(row_apply.reshape(rows), 'col')]
    all_gather x0 -> x4, blocking collectives: none -> 198 us  [local(): row_total = jnp.sum(lax.all_gather(row_apply.reshape(rows), 'col'), axis=0)]
  transfers between devices with their start and end apart: 3 -> 3, of which waited for: 0 -> 0; matrix products, arithmetic and copies ran while one was open for 0% -> 1% of each run, Pallas kernels for 0% -> 0%
where the time goes in v1:
time: 931 us; the launch traced here: 930 us
  blocking collectives  822 us (88%)
  matrix products  65.2 us (7%)
  between operations  17.4 us (2%)
  other arithmetic  13.3 us (1%)
    psum x1, blocking collectives, local(): lax.psum((jnp.sum(own_wts), jnp.sum(own_wts * phi_own)), ('row', 'col'))  343 us
    all_gather x4, blocking collectives, local(): row_total = jnp.sum(lax.all_gather(row_apply.reshape(rows), 'col'), axis=0)  198 us
    psum x1, blocking collectives, local(): lax.psum((rowmass_part.reshape(rows), rowph_part.reshape(rows)), 'col')  135 us
    unnamed x2, blocking collectives  85.5 us
    psum x3, blocking collectives, local(): col_total = lax.psum(col_apply, 'row')  27.5 us
    dot_general x48, matrix products, plan_only(): jnp.einsum('rd,cd->rc', part_blk, col_parts, preferred_element_type=jnp.f...  19.1 us
  transfers between devices with their start and end apart: 3, of which 0 were waited for; matrix products, arithmetic and copies ran while one was open for 1% of the time, Pallas kernels for 0%

profile of v1, /device:TPU:8, one launch (start us, length us, event | category | flops | bytes accessed | tf_op | source)
XLA Modules:
  0.0 930.5 jit_solution(11123894725908066340)
XLA Ops:
  7.2 0.7 all-gather.6.cloned.1.call-update
  8.0 1.3 dynamic-slice
  9.9 0.9 dynamic-update-slice
  10.7 75.0 %all-reduce = bf16[3072]{0:T(1024)(128)(2,1)S(1)} all-reduce(bf16[3072]{0:T(1024)(128)(2,1)S(1)} %dynamic-update-slice), channel_id=1, replica_groups=mesh['filt'=2,'row'=4,'col'=32] {'col'}, use_global_device_ids=true, to_apply=%add | all-reduce | flops 3072 | bytes 12288
  85.8 1.3 dynamic-slice.1
  87.6 0.9 dynamic-update-slice.1
  88.5 10.5 %all-reduce.1 = bf16[384]{0:T(512)(128)(2,1)S(1)} all-reduce(bf16[384]{0:T(512)(128)(2,1)S(1)} %dynamic-update-slice.1), channel_id=1, replica_groups=mesh['filt'=2,'row'=4,'col'=32] {'row'}, use_global_device_ids=true, to_apply=%add.1 | all-reduce | flops 384 | bytes 1536
  99.0 12.3 %all_gather.30 = bf16[384,256]{1,0:T(8,128)(2,1)S(1)} all-gather(bf16[96,256]{1,0:T(8,128)(2,1)} %param.25), channel_id=1, replica_groups=mesh['filt'=2,'row'=4,'col'=32] {'row'}, dimensions={0}, use_global_device_ids=true | all-gather | bytes 245760 | tf_op jit(solution)/shard_map/all_gather | solution.py:17
  111.3 12.3 %all_gather.31 = bf16[384,256]{1,0:T(8,128)(2,1)S(1)} all-gather(bf16[96,256]{1,0:T(8,128)(2,1)} %param.26), channel_id=1, replica_groups=mesh['filt'=2,'row'=4,'col'=32] {'row'}, dimensions={0}, use_global_device_ids=true | all-gather | bytes 245760 | tf_op jit(solution)/shard_map/all_gather | solution.py:18
  123.9 2.0 multiply_reduce_fusion
  125.9 7.0 while.118
  132.9 7.5 while.117
  133.4 0.8 fusion.226
  134.6 0.8 fusion.226
  135.9 0.8 fusion.226
  137.1 0.8 fusion.226
  138.4 0.8 fusion.226
  139.6 0.8 fusion.226
  140.5 51.0 %all-gather = f32[32,1,3072]{2,1,0:T(1,128)S(1)} all-gather(f32[1,1,3072]{2,1,0:T(1,128)S(1)} %reshape.119), channel_id=1, replica_groups=mesh['filt'=2,'row'=4,'col'=32] {'col'}, dimensions={0}, use_global_device_ids=true | all-gather | bytes 405504 | tf_op jit(solution)/shard_map/all_gather | solution.py:73
  191.5 134.8 %all-reduce.3 = (f32[3072]{0:T(1024)S(1)}, f32[3072]{0:T(1024)S(1)}) all-reduce(f32[3072]{0:T(1024)S(1)} %reshape.106, f32[3072]{0:T(1024)S(1)} %reshape.105), channel_id=1, replica_groups=mesh['filt'=2,'row'=4,'col'=32] {'col'}, use_global_device_ids=true, to_apply=%region_13.14 | all-reduce | flops 6144 | bytes 49152 | tf_op jit(solution)/shard_map/psum | solution.py:62
  326.6 5.8 while.119
  332.4 8.0 all-reduce.4
  340.9 7.5 while.124
  341.3 0.8 fusion.268
  342.6 0.8 fusion.268
  343.8 0.8 fusion.268
  345.1 0.8 fusion.268
  346.3 0.8 fusion.268
  347.6 0.8 fusion.268
  348.4 51.7 %all-gather.1 = f32[32,1,3072]{2,1,0:T(1,128)S(1)} all-gather(f32[1,1,3072]{2,1,0:T(1,128)S(1)} %reshape.121), channel_id=1, replica_groups=mesh['filt'=2,'row'=4,'col'=32] {'col'}, dimensions={0}, use_global_device_ids=true | all-gather | bytes 405504 | tf_op jit(solution)/shard_map/all_gather | solution.py:73
  400.4 5.8 while.120
  406.2 9.8 %psum.82 = f32[384]{0:T(512)S(1)} all-reduce(f32[384]{0:T(512)S(1)} %get-tuple-element.508), channel_id=1, replica_groups=mesh['filt'=2,'row'=4,'col'=32] {'row'}, use_global_device_ids=true, to_apply=%region_23.24 | all-reduce | flops 384 | bytes 3072 | tf_op jit(solution)/shard_map/psum | solution.py:81
  416.6 7.5 while.125
  417.0 0.8 fusion.274
  418.3 0.8 fusion.274
  419.5 0.8 fusion.274
  420.8 0.8 fusion.274
  422.0 0.8 fusion.274
  423.3 0.8 fusion.274
  424.1 46.2 %all-gather.2 = f32[32,1,3072]{2,1,0:T(1,128)S(1)} all-gather(f32[1,1,3072]{2,1,0:T(1,128)S(1)} %reshape.123), channel_id=1, replica_groups=mesh['filt'=2,'row'=4,'col'=32] {'col'}, dimensions={0}, use_global_device_ids=true | all-gather | bytes 405504 | tf_op jit(solution)/shard_map/all_gather | solution.py:73
  470.6 5.8 while.121
  476.3 8.0 psum.83
  484.9 7.5 while.126
  485.3 0.8 fusion.280
  486.6 0.8 fusion.280
  487.8 0.8 fusion.280
  489.1 0.8 fusion.280
  490.3 0.8 fusion.280
  491.6 0.8 fusion.280
  492.4 49.4 %all-gather.3 = f32[32,1,3072]{2,1,0:T(1,128)S(1)} all-gather(f32[1,1,3072]{2,1,0:T(1,128)S(1)} %reshape.125), channel_id=1, replica_groups=mesh['filt'=2,'row'=4,'col'=32] {'col'}, dimensions={0}, use_global_device_ids=true | all-gather | bytes 405504 | tf_op jit(solution)/shard_map/all_gather | solution.py:73
  542.2 5.8 while.122
  548.0 9.7 %psum.84 = f32[384]{0:T(512)S(1)} all-reduce(f32[384]{0:T(512)S(1)} %get-tuple-element.512), channel_id=1, replica_groups=mesh['filt'=2,'row'=4,'col'=32] {'row'}, use_global_device_ids=true, to_apply=%region_35.36 | all-reduce | flops 384 | bytes 3072 | tf_op jit(solution)/shard_map/psum | solution.py:81
  557.7 16.9 %while.123 = (s32[]{:T(128)}, f32[384,256]{1,0:T(8,128)S(1)}, bf16[6,512,256]{2,1,0:T(8,128)(2,1)}, f32[6,512]{1,0:T(8,128)S(1)}, f32[384]{0:T(512)S(1)}, /*inde...) while((s32[]{:T(128)}, f32[384,256]{1,0:T(8,128)S(1)}, ...), condition=%wide.region_38.39_spmd.clone, body=%wide.region_36.38_spmd.clone.sunk | while | flops 508100096 | bytes 9079975 | solution.py:102
  559.1 1.0 fusion.262
  562.0 1.0 fusion.262
  564.8 1.0 fusion.262
  567.6 1.0 fusion.262
  570.4 1.0 fusion.262
  573.2 1.0 fusion.262
  574.7 0.7 convert_element_type.46
  575.4 0.7 all-reduce.7.cloned.1.call-update
  576.1 0.7 convert_reduce_fusion
  576.8 343.0 %all-reduce.2 = (f32[]{:T(128)}, f32[]{:T(128)}) all-reduce(f32[]{:T(128)} %get-tuple-element.718, f32[]{:T(128)} %get-tuple-element.717), channel_id=1, replica_groups=mesh['filt'=2,'row'=4,'col'=32] {'row','col'}, use_global_device_ids=true, to_apply=%region_44.45 | all-reduce | flops 2 | bytes 16 | tf_op jit(solution)/shard_map/psum | solution.py:115
  922.5 1.5 add_convert_fusion
  (311 shorter events, 54.1 us)
Async XLA Ops:
  7.2 116.7 %all-gather.6.cloned.1.call-start = ((), (), s32[]{:S(2)}) async-start(), calls=%async_computation.1 | async-start | bytes 1622016 | tf_op jit(solution)/shard_map/all_gather | solution.py:12
  7.9 914.6 %reduce-scatter.2.cloned.1.call-start = ((), (), s32[]{:S(2)}) async-start(), calls=%async_computation.3 | async-start | bytes 245760 | tf_op jit(solution)/shard_map/reduce_scatter | solution.py:109
  123.8 2.1 copy-start
  340.3 0.6 copy-start.1
  416.0 0.6 copy-start.2
  484.3 0.6 copy-start.3
  574.7 1.5 copy-start.4
  575.4 347.1 %all-reduce.7.cloned.1.call-start = ((), (), s32[]{:S(2)}) async-start(), calls=%async_computation.2 | async-start | bytes 3145728 | tf_op jit(solution)/shard_map/psum | solution.py:107
Sparse Core Ops, SparseCore 0:
  10.6 78.8 all-gather.5
  575.5 17.6 reduce-scatter.1
  597.0 150.1 all-reduce.6
